TPU v7x, 32 devices: a whole 2x2x4 slice. The times are simulated.
32 devices in a mesh: dom: 8 (over z, core), grp: 4 (over y, x).
Axes of the slice: x: 2, y: 2, z: 4, core: 2. Of those that a mesh axis runs over, the one named last changes fastest.
Arguments:
- feats: bfloat16 [8192, 256], P(('dom', 'grp')), may hold values from -6 to 6
- w_self: bfloat16 [256, 256], replicated, may hold values from -0.375 to 0.375
- w_neigh: bfloat16 [256, 256], replicated, may hold values from -0.375 to 0.375
- local_tiles: bfloat16 [64, 3, 128, 128], P(('dom', 'grp')), may hold values from -0.15625 to 0.15625
- local_cols: int32 [64, 3], P(('dom', 'grp')), may hold values from 0 to 7, as said below
- cut_tiles: bfloat16 [64, 10, 128, 128], P(('dom', 'grp')), may hold values from -0.15625 to 0.15625
- cut_src: int32 [64, 10], P(('dom', 'grp')), may hold values from 0 to 7, as said below
- send_block: int32 [32, 8], P(('dom', 'grp')), may hold values from 0 to 1
- send_live: int32 [32, 8], P(('dom', 'grp')), may hold values from 0 to 1, as said below
- cotangent: bfloat16 [8192, 256], P(('dom', 'grp')), may hold values from -0.0625 to 0.0625
Outputs:
- layer_out: bfloat16 [8192, 256], P(('dom', 'grp'))
- grad_self: float32 [256, 256], replicated
- grad_neigh: float32 [256, 256], replicated
Inputs may be any that keep to these rules, and one draw needn't show every extreme that they name: `local_cols`: the 3 column blocks of one row block are distinct. `cut_src`: 0 marks an empty slot; the share of filled slots differs from partition to partition. send_live[e, p] is 1 exactly when some row block of device p * 4 + g (g the position of e) has a cut slot with offset naming e's partition; it is 0 where p is e's own partition.
All inputs are finite; a program needn't handle non-finite values.
Results may differ from a plain program's by a relative error of at most 0.0056.
Values may be sent and summed in bfloat16 or wider, within the bound.
A program may use at most 64 MiB of HBM per device.

v0:
```python
import jax
import jax.numpy as jnp
from jax import lax
from jax.sharding import PartitionSpec as P


def body(
    feats,
    w_self,
    w_neigh,
    local_tiles,
    local_cols,
    cut_tiles,
    cut_src,
    send_block,
    send_live,
    cotangent,
):
    row_blocks = local_tiles.shape[0]
    block_size = local_tiles.shape[2]
    features = feats.shape[1]
    partitions = lax.axis_size("dom")
    own_blocks = feats.reshape(row_blocks, block_size, features)
    gathered = lax.all_gather(feats, "grp", axis=0, tiled=True)
    picked = gathered.reshape(-1, block_size, features)[local_cols]
    aggregate_sum = jnp.einsum(
        "rkij,rkjf->rif", local_tiles, picked, preferred_element_type=jnp.float32
    )
    outgoing = own_blocks[send_block[0]] * send_live[0][:, None, None].astype(jnp.bfloat16)
    received = lax.all_to_all(outgoing, "dom", split_axis=0, concat_axis=0, tiled=True)
    source = (lax.axis_index("dom") + cut_src) % partitions
    remote = received[source]
    aggregate_sum = aggregate_sum + jnp.einsum(
        "rkij,rkjf->rif", cut_tiles, remote, preferred_element_type=jnp.float32
    )
    agg = aggregate_sum.reshape(row_blocks * block_size, features).astype(jnp.bfloat16)
    preact = jnp.dot(feats, w_self, preferred_element_type=jnp.float32) + jnp.dot(
        agg, w_neigh, preferred_element_type=jnp.float32
    )
    sigmoid = jax.nn.sigmoid(preact)
    layer_out = (preact * sigmoid).astype(jnp.bfloat16)
    grad_pre = (cotangent.astype(jnp.float32) * sigmoid * (1.0 + preact * (1.0 - sigmoid))).astype(
        jnp.bfloat16
    )
    grad_own = jnp.dot(feats.T, grad_pre, preferred_element_type=jnp.float32)
    grad_agg = jnp.dot(agg.T, grad_pre, preferred_element_type=jnp.float32)
    stacked = jnp.concatenate([grad_own, grad_agg], axis=0)
    shared = lax.psum_scatter(stacked, "grp", scatter_dimension=0, tiled=True)
    shared = lax.psum(shared, "dom")
    summed = lax.all_gather(shared, "grp", axis=0, tiled=True)
    return (layer_out, summed[:features], summed[features:])


def solution(mesh):
    return jax.shard_map(
        body,
        mesh=mesh,
        in_specs=(
            P(("dom", "grp"), None),
            P(),
            P(),
            P(("dom", "grp"), None, None, None),
            P(("dom", "grp"), None),
            P(("dom", "grp"), None, None, None),
            P(("dom", "grp"), None),
            P(("dom", "grp"), None),
            P(("dom", "grp"), None),
            P(("dom", "grp"), None),
        ),
        out_specs=(P(("dom", "grp"), None), P(), P()),
        check_vma=False,
    )
```

profile of v0, /device:TPU:0, one launch (start us, length us, event | category | flops | bytes accessed | tf_op | source)
XLA Modules:
  0.0 135.9 jit_solution(555693463951138174)
XLA Ops:
  7.2 0.0 copy-start
  7.2 0.7 fusion.3
  7.9 0.7 convert_bitcast_fusion
  8.6 1.5 %gather_fusion.1 = bf16[8,128,256]{2,1,0:T(8,128)(2,1)S(1)} fusion(bf16[2,128,256]{2,1,0:T(8,128)(2,1)} %bitcast.37, s32[1024]{0:T(1024)S(1)} %pad_clamp_fusion.1), kind=kCustom, calls=%fused_computation.1 | custom fusion | bytes 1048608 | tf_op jit(solution)/shard_map/gather | solution.py:29
  10.1 0.0 copy-start.4
  10.1 0.0 copy-start.5
  10.1 0.9 broadcast_multiply_fusion
  11.0 6.5 %all-to-all-start = ((bf16[8,128,256]{2,1,0:T(8,128)(2,1)}), bf16[8,128,256]{2,1,0:T(8,128)(2,1)S(1)}, u32[]{:S(2)}, u32[]{:S(2)}) async-start(bf16[8,128,256]{2,1,0:T(8,128)(2,1)} %broadcast_multiply_fusion), calls=%async_computation | async-start | bytes 1048576 | tf_op jit(solution)/shard_map/all_to_all | solution.py:30
  17.5 0.0 reduce-scatter.2.cloned.1.call-start
  17.6 0.1 reshape.70
  17.6 0.1 reshape.54
  17.7 10.6 %all_gather.6 = bf16[1024,256]{1,0:T(8,128)(2,1)S(1)} all-gather(bf16[256,256]{1,0:T(8,128)(2,1)S(1)} %copy-done.1), channel_id=1, replica_groups=mesh['dom'=8,'grp'=4] {'grp'}, dimensions={0}, use_global_device_ids=true | all-gather | bytes 655360 | tf_op jit(solution)/shard_map/all_gather | solution.py:24
  28.3 0.6 gather_fusion
  28.9 0.2 convolution_bitcast_fusion
  29.2 0.2 fusion.5
  29.4 3.5 %all-to-all-done = bf16[8,128,256]{2,1,0:T(8,128)(2,1)S(1)} async-done(((bf16[8,128,256]{2,1,0:T(8,128)(2,1)}), bf16[8,128,256]{2,1,0:T(8,128)(2,1)S(1)}, u32[]{:S(2)}, u32[]{:S(2)}) %all-to-all-start) | async-done | bytes 524320 | tf_op jit(solution)/shard_map/all_to_all | solution.py:30
  32.8 0.6 gather_fusion.2
  33.5 0.0 copy-start.7
  33.5 0.3 fusion.1
  33.9 0.5 copy-done.6
  34.4 0.1 copy-done.7
  34.4 0.9 multiply_convert_fusion
  35.4 0.2 fusion.6
  35.6 0.2 convolution_bitcast_fusion.1
  35.8 0.8 pad_maximum_fusion
  36.7 0.0 reduce-scatter.2.cloned.1.call-update
  36.7 0.0 all-reduce.2.cloned.1.call-start
  36.8 23.8 %reduce-scatter.2.cloned.1.call-done = f32[128,256]{1,0:T(8,128)} async-done(((f32[512,256]{1,0:T(8,128)}), f32[128,256]{1,0:T(8,128)}) %reduce-scatter.2.cloned.1.call-update) | async-done | bytes 131088 | tf_op jit(solution)/shard_map/reduce_scatter | solution.py:48
  60.5 0.0 all-reduce.2.cloned.1.call-update
  60.6 56.7 %all-reduce.2.cloned.1.call-done = f32[128,256]{1,0:T(8,128)} async-done(((f32[128,256]{1,0:T(8,128)}), f32[128,256]{1,0:T(8,128)}) %all-reduce.2.cloned.1.call-update) | async-done | bytes 131088 | tf_op jit(solution)/shard_map/psum | solution.py:49
  117.2 11.0 %all_gather.7 = f32[512,256]{1,0:T(8,128)S(1)} all-gather(f32[128,256]{1,0:T(8,128)} %all-reduce.2.cloned.1.call-done), channel_id=1, replica_groups=mesh['dom'=8,'grp'=4] {'grp'}, dimensions={0}, use_global_device_ids=true | all-gather | bytes 655360 | tf_op jit(solution)/shard_map/all_gather | solution.py:50
  128.3 0.8 fusion.4
  (15 shorter events, 0.1 us)
Async XLA Ops:
  7.2 26.3 %copy-start = (bf16[2,10,128,128]{3,2,1,0:T(8,128)(2,1)S(1)}, bf16[2,10,128,128]{3,2,1,0:T(8,128)(2,1)}, u32[]{:S(2)}) copy-start(bf16[2,10,128,128]{3,2,1,0:T(8,128)(2,1)} %param.15) | copy-start | bytes 1966084
  10.1 7.5 %copy-start.4 = (s32[2,10]{1,0:T(2,128)S(1)}, s32[2,10]{1,0:T(2,128)}, u32[]{:S(2)}) copy-start(s32[2,10]{1,0:T(2,128)} %param.16) | copy-start | bytes 244
  10.1 7.6 %copy-start.5 = (s32[2,3]{1,0:T(2,128)S(1)}, s32[2,3]{1,0:T(2,128)}, u32[]{:S(2)}) copy-start(s32[2,3]{1,0:T(2,128)} %param.14) | copy-start | bytes 76
  10.1 7.6 %copy-start.1 = (bf16[256,256]{1,0:T(8,128)(2,1)S(1)}, bf16[256,256]{1,0:T(8,128)(2,1)}, u32[]{:S(2)}) copy-start(bf16[256,256]{1,0:T(8,128)(2,1)} %param.10) | copy-start | bytes 393220
  11.0 17.9 %copy-start.2 = (bf16[2,3,128,128]{3,2,1,0:T(8,128)(2,1)S(1)}, bf16[2,3,128,128]{3,2,1,0:T(8,128)(2,1)}, u32[]{:S(2)}) copy-start(bf16[2,3,128,128]{3,2,1,0:T(8,128)(2,1)} %param.13) | copy-start | bytes 589828
  11.0 21.8 %all-to-all-start = ((bf16[8,128,256]{2,1,0:T(8,128)(2,1)}), bf16[8,128,256]{2,1,0:T(8,128)(2,1)S(1)}, u32[]{:S(2)}, u32[]{:S(2)}) async-start(bf16[8,128,256]{2,1,0:T(8,128)(2,1)} %broadcast_multiply_fusion), calls=%async_computation | async-start | bytes 1048576 | tf_op jit(solution)/shard_map/all_to_all | solution.py:30
  17.5 11.7 %copy-start.3 = (bf16[256,256]{1,0:T(8,128)(2,1)S(1)}, bf16[256,256]{1,0:T(8,128)(2,1)}, u32[]{:S(2)}) copy-start(bf16[256,256]{1,0:T(8,128)(2,1)} %param.11) | copy-start | bytes 393220
  17.5 43.1 %reduce-scatter.2.cloned.1.call-start = ((), (), s32[]{:S(2)}) async-start(), calls=%async_computation.2 | async-start | bytes 655360 | tf_op jit(solution)/shard_map/reduce_scatter | solution.py:48
  33.5 0.9 copy-start.6
  33.5 1.0 copy-start.7
  36.7 80.5 %all-reduce.2.cloned.1.call-start = ((), (), s32[]{:S(2)}) async-start(), calls=%async_computation.3 | async-start | bytes 262144 | tf_op jit(solution)/shard_map/psum | solution.py:49
Sparse Core Ops, SparseCore 0:
  36.8 23.6 reduce-scatter.1
  63.0 54.2 all-reduce.1
where the time goes:
time: 136 us
  waiting for transfers between devices  84 us (62%)
  blocking collectives  21.6 us (16%)
  between operations  14.2 us (10%)
  starting transfers between devices  6.54 us (5%)
  local copies, waits for them, and re-layouts  4.3 us (3%)
  other arithmetic  3.17 us (2%)
  matrix products  2.14 us (2%)
    psum x1, waiting for transfers between devices, body(): shared = lax.psum(shared, 'dom')  56.7 us
    reduce_scatter x1, waiting for transfers between devices, body(): shared = lax.psum_scatter(stacked, 'grp', scatter_dimension=0, tiled=True)  23.8 us
    all_gather x1, blocking collectives, body(): summed = lax.all_gather(shared, 'grp', axis=0, tiled=True)  11 us
    all_gather x1, blocking collectives, body(): gathered = lax.all_gather(feats, 'grp', axis=0, tiled=True)  10.6 us
    all_to_all x1, starting transfers between devices, body(): lax.all_to_all(outgoing, 'dom', split_axis=0, concat_axis=0, tiled=True)  6.46 us
    all_to_all x1, waiting for transfers between devices, body(): lax.all_to_all(outgoing, 'dom', split_axis=0, concat_axis=0, tiled=True)  3.46 us
  transfers between devices with their start and end apart: 3, of which 3 were waited for; matrix products, arithmetic and copies ran while one was open for 1% of the time, Pallas kernels for 0%

commit v1 on v0

--- a/solution.py
+++ b/solution.py
@@ -46,7 +46,7 @@
     grad_agg = jnp.dot(agg.T, grad_pre, preferred_element_type=jnp.float32)
     stacked = jnp.concatenate([grad_own, grad_agg], axis=0)
     shared = lax.psum_scatter(stacked, "grp", scatter_dimension=0, tiled=True)
-    shared = lax.psum(shared, "dom")
+    shared = jnp.sum(lax.all_gather(shared, "dom"), axis=0)
     summed = lax.all_gather(shared, "grp", axis=0, tiled=True)
     return (layer_out, summed[:features], summed[features:])
 

time: 136 us -> 104 us (0.76)
  waiting for transfers between devices: 84 us -> 51.1 us
    psum x1 -> x0, waiting for transfers between devices: 56.7 us -> none  [body(): shared = lax.psum(shared, 'dom')]
    all_gather x0 -> x1, waiting for transfers between devices: none -> 23.8 us  [body(): shared = jnp.sum(lax.all_gather(shared, 'dom'), axis=0)]
where the time goes in v1:
time: 104 us; the launch traced here: 103 us
  waiting for transfers between devices  51.1 us (49%)
  blocking collectives  20.6 us (20%)
  between operations  14.2 us (14%)
  starting transfers between devices  6.54 us (6%)
  other arithmetic  4.47 us (4%)
  local copies, waits for them, and re-layouts  4.3 us (4%)
  matrix products  2.14 us (2%)
    reduce_scatter x1, waiting for transfers between devices, body(): shared = lax.psum_scatter(stacked, 'grp', scatter_dimension=0, tiled=True)  23.8 us
    all_gather x1, waiting for transfers between devices, body(): shared = jnp.sum(lax.all_gather(shared, 'dom'), axis=0)  23.8 us
    all_gather x1, blocking collectives, body(): gathered = lax.all_gather(feats, 'grp', axis=0, tiled=True)  10.6 us
    all_gather x1, blocking collectives, body(): summed = lax.all_gather(shared, 'grp', axis=0, tiled=True)  9.99 us
    all_to_all x1, starting transfers between devices, body(): lax.all_to_all(outgoing, 'dom', split_axis=0, concat_axis=0, tiled=True)  6.46 us
    all_to_all x1, waiting for transfers between devices, body(): lax.all_to_all(outgoing, 'dom', split_axis=0, concat_axis=0, tiled=True)  3.46 us
  transfers between devices with their start and end apart: 3, of which 3 were waited for; matrix products, arithmetic and copies ran while one was open for 1% of the time, Pallas kernels for 0%

profile of v1, /device:TPU:0, one launch (start us, length us, event | category | flops | bytes accessed | tf_op | source)
XLA Modules:
  0.0 103.3 jit_solution(526052333743112662)
XLA Ops:
  7.2 0.0 copy-start
  7.2 0.7 fusion.3
  7.9 0.7 convert_bitcast_fusion
  8.6 1.5 %gather_fusion.1 = bf16[8,128,256]{2,1,0:T(8,128)(2,1)S(1)} fusion(bf16[2,128,256]{2,1,0:T(8,128)(2,1)} %bitcast.38, s32[1024]{0:T(1024)S(1)} %pad_clamp_fusion.1), kind=kCustom, calls=%fused_computation.1 | custom fusion | bytes 1048608 | tf_op jit(solution)/shard_map/gather | solution.py:29
  10.1 0.0 copy-start.4
  10.1 0.9 broadcast_multiply_fusion
  11.0 6.5 %all-to-all-start = ((bf16[8,128,256]{2,1,0:T(8,128)(2,1)}), bf16[8,128,256]{2,1,0:T(8,128)(2,1)S(1)}, u32[]{:S(2)}, u32[]{:S(2)}) async-start(bf16[8,128,256]{2,1,0:T(8,128)(2,1)} %broadcast_multiply_fusion), calls=%async_computation | async-start | bytes 1048576 | tf_op jit(solution)/shard_map/all_to_all | solution.py:30
  17.5 0.0 reduce-scatter.2.cloned.1.call-start
  17.6 0.1 reshape.70
  17.6 0.1 reshape.54
  17.7 10.6 %all_gather.12 = bf16[1024,256]{1,0:T(8,128)(2,1)S(1)} all-gather(bf16[256,256]{1,0:T(8,128)(2,1)S(1)} %copy-done.1), channel_id=1, replica_groups=mesh['dom'=8,'grp'=4] {'grp'}, dimensions={0}, use_global_device_ids=true | all-gather | bytes 655360 | tf_op jit(solution)/shard_map/all_gather | solution.py:24
  28.3 0.6 gather_fusion
  28.9 0.2 convolution_bitcast_fusion
  29.2 0.2 fusion.5
  29.4 3.5 %all-to-all-done = bf16[8,128,256]{2,1,0:T(8,128)(2,1)S(1)} async-done(((bf16[8,128,256]{2,1,0:T(8,128)(2,1)}), bf16[8,128,256]{2,1,0:T(8,128)(2,1)S(1)}, u32[]{:S(2)}, u32[]{:S(2)}) %all-to-all-start) | async-done | bytes 524320 | tf_op jit(solution)/shard_map/all_to_all | solution.py:30
  32.8 0.6 gather_fusion.2
  33.5 0.0 copy-start.7
  33.5 0.3 fusion.1
  33.9 0.5 copy-done.6
  34.4 0.1 copy-done.7
  34.4 0.9 multiply_convert_fusion
  35.4 0.2 fusion.6
  35.6 0.2 convolution_bitcast_fusion.1
  35.8 0.8 pad_maximum_fusion
  36.7 0.0 reduce-scatter.2.cloned.1.call-update
  36.7 0.0 all-gather.3.cloned.1.call-start
  36.8 23.8 %reduce-scatter.2.cloned.1.call-done = f32[128,256]{1,0:T(8,128)} async-done(((f32[512,256]{1,0:T(8,128)}), f32[128,256]{1,0:T(8,128)}) %reduce-scatter.2.cloned.1.call-update) | async-done | bytes 131088 | tf_op jit(solution)/shard_map/reduce_scatter | solution.py:48
  60.6 0.0 all-gather.3.cloned.1.call-update
  60.6 23.8 %all-gather.3.cloned.1.call-done = f32[1024,256]{1,0:T(8,128)} async-done(((f32[128,256]{1,0:T(8,128)}), f32[1024,256]{1,0:T(8,128)}) %all-gather.3.cloned.1.call-update) | async-done | bytes 1048592 | tf_op jit(solution)/shard_map/all_gather | solution.py:49
  84.4 1.3 %reduce_sum.9 = f32[128,256]{1,0:T(8,128)S(1)} reduce(f32[8,128,256]{2,1,0:T(8,128)} %bitcast.42, f32[]{:T(128)} %constant.31.clone.1), dimensions={0}, to_apply=%region_1.2 | reduce | flops 229376 | bytes 1179652 | tf_op jit(solution)/shard_map/reduce_sum | solution.py:49
  85.7 10.0 %all_gather.15 = f32[512,256]{1,0:T(8,128)S(1)} all-gather(f32[128,256]{1,0:T(8,128)S(1)} %reduce_sum.9), channel_id=1, replica_groups=mesh['dom'=8,'grp'=4] {'grp'}, dimensions={0}, use_global_device_ids=true | all-gather | bytes 655360 | tf_op jit(solution)/shard_map/all_gather | solution.py:50
  95.7 0.8 fusion.4
  (16 shorter events, 0.1 us)
Async XLA Ops:
  7.2 26.3 %copy-start = (bf16[2,10,128,128]{3,2,1,0:T(8,128)(2,1)S(1)}, bf16[2,10,128,128]{3,2,1,0:T(8,128)(2,1)}, u32[]{:S(2)}) copy-start(bf16[2,10,128,128]{3,2,1,0:T(8,128)(2,1)} %param.15) | copy-start | bytes 1966084
  10.1 7.5 %copy-start.4 = (s32[2,10]{1,0:T(2,128)S(1)}, s32[2,10]{1,0:T(2,128)}, u32[]{:S(2)}) copy-start(s32[2,10]{1,0:T(2,128)} %param.16) | copy-start | bytes 244
  10.1 7.6 %copy-start.5 = (s32[2,3]{1,0:T(2,128)S(1)}, s32[2,3]{1,0:T(2,128)}, u32[]{:S(2)}) copy-start(s32[2,3]{1,0:T(2,128)} %param.14) | copy-start | bytes 76
  10.1 7.6 %copy-start.1 = (bf16[256,256]{1,0:T(8,128)(2,1)S(1)}, bf16[256,256]{1,0:T(8,128)(2,1)}, u32[]{:S(2)}) copy-start(bf16[256,256]{1,0:T(8,128)(2,1)} %param.10) | copy-start | bytes 393220
  11.0 17.9 %copy-start.2 = (bf16[2,3,128,128]{3,2,1,0:T(8,128)(2,1)S(1)}, bf16[2,3,128,128]{3,2,1,0:T(8,128)(2,1)}, u32[]{:S(2)}) copy-start(bf16[2,3,128,128]{3,2,1,0:T(8,128)(2,1)} %param.13) | copy-start | bytes 589828
  11.0 21.8 %all-to-all-start = ((bf16[8,128,256]{2,1,0:T(8,128)(2,1)}), bf16[8,128,256]{2,1,0:T(8,128)(2,1)S(1)}, u32[]{:S(2)}, u32[]{:S(2)}) async-start(bf16[8,128,256]{2,1,0:T(8,128)(2,1)} %broadcast_multiply_fusion), calls=%async_computation | async-start | bytes 1048576 | tf_op jit(solution)/shard_map/all_to_all | solution.py:30
  17.5 11.7 %copy-start.3 = (bf16[256,256]{1,0:T(8,128)(2,1)S(1)}, bf16[256,256]{1,0:T(8,128)(2,1)}, u32[]{:S(2)}) copy-start(bf16[256,256]{1,0:T(8,128)(2,1)} %param.11) | copy-start | bytes 393220
  17.5 43.1 %reduce-scatter.2.cloned.1.call-start = ((), (), s32[]{:S(2)}) async-start(), calls=%async_computation.2 | async-start | bytes 655360 | tf_op jit(solution)/shard_map/reduce_scatter | solution.py:48
  33.5 0.9 copy-start.6
  33.5 1.0 copy-start.7
  36.7 47.7 %all-gather.3.cloned.1.call-start = ((), (), s32[]{:S(2)}) async-start(), calls=%async_computation.3 | async-start | bytes 1179648 | tf_op jit(solution)/shard_map/all_gather | solution.py:49
Sparse Core Ops, SparseCore 0:
  36.8 23.7 reduce-scatter.1
  62.3 22.0 all-gather.2
